TPU v7x, 32 devices: a whole 2x2x4 slice. The times are simulated.
32 devices in a mesh: dp: 16 (over z, y, x), grp: 2 (over core).
Axes of the slice: x: 2, y: 2, z: 4, core: 2. Of those that a mesh axis runs over, the one named last changes fastest.
Arguments:
- query_features: bfloat16 [32768, 512], P(('dp', 'grp')), may hold values from -256 to 256
- query_weights: bfloat16 [32768], P(('dp', 'grp')), may hold values from 0.5 to 13.5, as said below
- positive_index: int32 [32768], P(('dp', 'grp')), may hold values from 0 to 511
- item_features: bfloat16 [512, 512], P(('dp', 'grp')), may hold values from -6 to 6
- item_ids: int32 [512], P(('dp', 'grp')), may hold values from 0 to 255
- item_logq: bfloat16 [512], P(('dp', 'grp')), may hold values from -14 to -11
- query_w_in: bfloat16 [512, 1024], replicated, may hold values from -0.25 to 0.25
- query_w_out: bfloat16 [1024, 256], replicated, may hold values from -0.1875 to 0.1875
- item_w_in: bfloat16 [512, 1024], replicated, may hold values from -0.25 to 0.25
- item_w_out: bfloat16 [1024, 256], replicated, may hold values from -0.1875 to 0.1875
Outputs:
- grad_query_w_in: float32 [512, 1024], replicated
- grad_query_w_out: float32 [1024, 256], replicated
- grad_item_w_in: float32 [512, 1024], replicated
- grad_item_w_out: float32 [1024, 256], replicated
Inputs may be any that keep to these rules, and one draw needn't show every extreme that they name: `query_weights`: positive weights. `item_ids`: an id may occur several times in the sample set.
All inputs are finite; a program needn't handle non-finite values.
Results may differ from a plain program's by a relative error of at most 0.013.
Values may be sent and summed in bfloat16 or wider, within the bound.
A program may use at most 128 MiB of HBM per device.

v0:
```python
import jax
import jax.numpy as jnp
from jax import lax
from jax.sharding import PartitionSpec as P

score_scale = 0.25
loss_scale = 1024.0


def silu_slope(values):
    gate = jax.nn.sigmoid(values)
    return gate * (1.0 + values * (1.0 - gate))


def tower(features, weight_in, weight_out):
    pre_act = jnp.dot(features, weight_in, preferred_element_type=jnp.float32)
    hidden = jax.nn.silu(pre_act).astype(jnp.bfloat16)
    embedding = jnp.dot(hidden, weight_out, preferred_element_type=jnp.float32).astype(jnp.bfloat16)
    return (pre_act, hidden, embedding)


def tower_back(features, pre_act, hidden, weight_out, embed_grad):
    grad_out = jnp.dot(hidden.T, embed_grad, preferred_element_type=jnp.float32)
    hidden_grad = jnp.dot(embed_grad, weight_out.T, preferred_element_type=jnp.float32)
    pre_grad = (hidden_grad * silu_slope(pre_act)).astype(jnp.bfloat16)
    grad_in = jnp.dot(features.T, pre_grad, preferred_element_type=jnp.float32)
    return (grad_in, grad_out)


def item_scores(query_rows, items, item_bias, item_codes, columns, positives, pos_codes):
    raw_scores = lax.dot_general(
        query_rows, items, (((1,), (1,)), ((), ())), preferred_element_type=jnp.float32
    )
    scores = score_scale * raw_scores - item_bias.astype(jnp.float32)[None, :]
    masked_hits = (item_codes[None, :] == pos_codes[:, None]) & (
        columns[None, :] != positives[:, None]
    )
    return jnp.where(masked_hits, -jnp.inf, scores)


def partial_stats(scores):
    row_max = jnp.maximum(jnp.max(scores, axis=1), -1e30)
    row_sum = jnp.sum(jnp.exp(scores - row_max[:, None]), axis=1)
    return (row_max, row_sum)


def finish(scores, row_max, row_sum, columns, positives, weights):
    probability = jnp.exp(scores - row_max[:, None]) / row_sum[:, None]
    target = (columns[None, :] == positives[:, None]).astype(jnp.float32)
    return (weights.astype(jnp.float32)[:, None] * (probability - target)).astype(jnp.bfloat16)


def positive_codes(every_code, positives):
    slots = jnp.arange(every_code.shape[0], dtype=jnp.int32)
    return jnp.sum(jnp.where(positives[:, None] == slots[None, :], every_code[None, :], 0), axis=1)


def on_device(
    query_features,
    query_weights,
    positive_index,
    item_features,
    item_ids,
    item_logq,
    query_w_in,
    query_w_out,
    item_w_in,
    item_w_out,
):
    weight_part = jnp.sum(query_weights.astype(jnp.float32))
    weight_total = lax.psum(weight_part, ("dp", "grp"))
    query_pre, query_hidden, query_embed = tower(query_features, query_w_in, query_w_out)
    item_pre, item_hidden, item_embed = tower(item_features, item_w_in, item_w_out)
    items_all, bias_all, codes_all = (
        lax.all_gather(item_embed, ("dp", "grp"), axis=0, tiled=True),
        lax.all_gather(item_logq, ("dp", "grp"), axis=0, tiled=True),
        lax.all_gather(item_ids, ("dp", "grp"), axis=0, tiled=True),
    )
    columns = jnp.arange(items_all.shape[0], dtype=jnp.int32)
    pos_codes = positive_codes(codes_all, positive_index)
    scores = item_scores(
        query_embed, items_all, bias_all, codes_all, columns, positive_index, pos_codes
    )
    row_max, row_sum = partial_stats(scores)
    dlogit = finish(scores, row_max, row_sum, columns, positive_index, query_weights)
    query_grad = (
        score_scale * jnp.dot(dlogit, items_all, preferred_element_type=jnp.float32)
    ).astype(jnp.bfloat16)
    item_grad = lax.psum_scatter(
        score_scale
        * lax.dot_general(
            dlogit, query_embed, (((0,), (0,)), ((), ())), preferred_element_type=jnp.float32
        ),
        ("dp", "grp"),
        scatter_dimension=0,
        tiled=True,
    ).astype(jnp.bfloat16)
    query_in_part, query_out_part = tower_back(
        query_features, query_pre, query_hidden, query_w_out, query_grad
    )
    item_in_part, item_out_part = tower_back(
        item_features, item_pre, item_hidden, item_w_out, item_grad
    )
    query_in_sum, query_out_sum, item_in_sum, item_out_sum = lax.psum(
        (query_in_part, query_out_part, item_in_part, item_out_part), ("dp", "grp")
    )
    factor = loss_scale / weight_total
    return (
        query_in_sum * factor,
        query_out_sum * factor,
        item_in_sum * factor,
        item_out_sum * factor,
    )


def solution(mesh):
    in_specs = (
        P(("dp", "grp"), None),
        P(("dp", "grp")),
        P(("dp", "grp")),
        P(("dp", "grp"), None),
        P(("dp", "grp")),
        P(("dp", "grp")),
        P(),
        P(),
        P(),
        P(),
    )
    out_specs = (P(), P(), P(), P())
    return jax.shard_map(
        on_device, mesh=mesh, in_specs=in_specs, out_specs=out_specs, check_vma=False
    )
```

profile of v0, /device:TPU:0, one launch (start us, length us, event | category | flops | bytes accessed | tf_op | source)
XLA Modules:
  0.0 457.4 jit_solution(10545431475410207212)
XLA Ops:
  7.2 1.6 fusion.16
  8.8 1.2 convolution_convert_fusion.1
  10.0 43.9 %all_gather.10 = bf16[512,256]{1,0:T(8,128)(2,1)S(1)} all-gather(bf16[16,256]{1,0:T(8,128)(2,1)S(1)} %convolution_convert_fusion.1), channel_id=1, replica_groups=mesh['dp'=16,'grp'=2] {'dp','grp'}, dimensions={0}, use_global_device_ids=true | all-gather | bytes 270336 | tf_op jit(solution)/shard_map/all_gather | solution.py:75
  54.0 0.8 dynamic-update-slice
  54.8 36.8 %all-reduce = s32[512]{0:T(512)S(1)} all-reduce(s32[512]{0:T(512)S(1)} %dynamic-update-slice), channel_id=1, replica_groups=mesh['dp'=16,'grp'=2] {'dp','grp'}, use_global_device_ids=true, to_apply=%add | all-reduce | flops 512 | bytes 4096
  91.6 0.8 dynamic-update-slice.1
  92.5 41.1 %all-reduce.1 = bf16[512]{0:T(512)(128)(2,1)S(1)} all-reduce(bf16[512]{0:T(512)(128)(2,1)S(1)} %dynamic-update-slice.1), channel_id=1, replica_groups=mesh['dp'=16,'grp'=2] {'dp','grp'}, use_global_device_ids=true, to_apply=%add.1 | all-reduce | flops 512 | bytes 2048
  133.6 4.8 %multiply_convert_fusion.1 = (bf16[1024,1024]{1,0:T(8,128)(2,1)S(1)}, f32[1024,1024]{1,0:T(8,128)}) fusion(bf16[1024,512]{1,0:T(8,128)(2,1)S(1)} %copy-done, bf16[512,1024]{1,0:T(8,128)(2,1)} %param.16), kind=kOutput, calls=%fused_computation.1 | convolution fusion | flops 1078984704 | bytes 8388608 | tf_op jit(solution)/shard_map/dot_general | solution.py:16
  138.4 0.7 convolution_convert_fusion
  140.0 0.8 fusion.15
  141.2 0.7 multiply_convert_fusion.2
  141.8 1.2 convolution_multiply_fusion.1
  143.7 1.1 copy-done.8
  144.7 1.7 fusion.17
  146.5 6.1 %convolution_bitcast_fusion.1 = f32[512,1024]{0,1:T(8,128)} fusion(bf16[1024,512]{1,0:T(8,128)(2,1)S(1)} %copy-done, f32[1024,1024]{1,0:T(8,128)} %get-tuple-element.13, bf16[1024,256]{1,0:T(8,128)(2,1)S(1)} %fusion.2, bf16[1024,256]{1,0:T(8,128)(2,1)S(1)} %copy-done.6), kind=kOutput, calls=%fused_computation.13 | convolution fusion | flops 1620049920 | bytes 8388608 | tf_op jit(solution)/shard_map/dot_general | solution.py:26
  152.5 126.6 %reduce-scatter.2.cloned.1.call-done = f32[16,256]{1,0:T(8,128)} async-done(((f32[512,256]{1,0:T(8,128)}), f32[16,256]{1,0:T(8,128)}) %reduce-scatter.2.cloned.1.call-update) | async-done | bytes 16400 | tf_op jit(solution)/shard_map/reduce_scatter | solution.py:89
  279.2 2.7 convolution_bitcast_fusion
  281.9 1.3 fusion.9
  283.9 38.4 %psum.36 = f32[]{:T(128)} all-reduce(f32[]{:T(128)} %convert_reduce_fusion), channel_id=1, replica_groups=mesh['dp'=16,'grp'=2] {'dp','grp'}, use_global_device_ids=true, to_apply=%region_5.6 | all-reduce | flops 1 | bytes 8 | tf_op jit(solution)/shard_map/psum | solution.py:71
  322.9 115.9 %all-reduce.5.cloned.1.call-done = (f32[512,1024]{0,1:T(8,128)}, f32[1024,256]{1,0:T(8,128)}, f32[512,1024]{0,1:T(8,128)}, f32[1024,256]{1,0:T(8,128)}) async-done(((f32[512,1024]{0,1:T(8,128)}, f32[1024,256]{1,0:T(8,128)}, f32[512,1024]{0,1:T(8,128)}, f32[1024,256]{1,0:T(8,128)}), (f32[512,1024]{0,1:T(8,128)}, f32[1024,256]{1,0:T(8,128)}, f32[512,1024]{0,1:T(8,128)}, ...) | async-done | bytes 6291472 | tf_op jit(solution)/shard_map/psum | solution.py:104
  438.8 4.0 broadcast_multiply_fusion
  442.9 2.9 copy.14
  445.8 1.8 copy.15
  447.6 3.0 broadcast_multiply_fusion.2
  (30 shorter events, 2.5 us)
Async XLA Ops:
  7.2 126.5 %copy-start = (bf16[1024,512]{1,0:T(8,128)(2,1)S(1)}, bf16[1024,512]{1,0:T(8,128)(2,1)}, u32[]{:S(2)}) copy-start(bf16[1024,512]{1,0:T(8,128)(2,1)} %param.10) | copy-start | bytes 3145732
  7.2 272.0 %reduce-scatter.2.cloned.1.call-start = ((), (), s32[]{:S(2)}) async-start(), calls=%async_computation.1 | async-start | bytes 540672 | tf_op jit(solution)/shard_map/reduce_scatter | solution.py:89
  133.6 4.8 %copy-start.6 = (bf16[1024,256]{1,0:T(8,128)(2,1)S(1)}, bf16[1024,256]{1,0:T(8,128)(2,1)}, u32[]{:S(2)}) copy-start(bf16[1024,256]{1,0:T(8,128)(2,1)} %param.17) | copy-start | bytes 1572868
  138.4 1.3 copy-start.7
  138.4 1.3 copy-start.4
  140.0 0.8 copy-start.5
  143.1 295.7 %all-reduce.5.cloned.1.call-start = ((), (), s32[]{:S(2)}) async-start(), calls=%async_computation.2 | async-start | bytes 12582912 | tf_op jit(solution)/shard_map/psum | solution.py:104
  143.2 1.6 copy-start.8
  146.5 132.7 %copy-start.1 = (bf16[1024,256]{1,0:T(8,128)(2,1)S(1)}, bf16[1024,256]{1,0:T(8,128)(2,1)}, u32[]{:S(2)}) copy-start(bf16[1024,256]{1,0:T(8,128)(2,1)} %param.19) | copy-start | bytes 1572868
  146.5 132.7 %copy-start.2 = (bf16[16,512]{1,0:T(8,128)(2,1)S(1)}, bf16[16,512]{1,0:T(8,128)(2,1)}, u32[]{:S(2)}) copy-start(bf16[16,512]{1,0:T(8,128)(2,1)} %param.13) | copy-start | bytes 49156
  279.2 2.8 copy-start.3
Sparse Core Ops, SparseCore 0:
  143.2 135.9 reduce-scatter.1
  285.8 153.0 all-reduce.4
where the time goes:
time: 458 us; the launch traced here: 457 us
  waiting for transfers between devices  243 us (53%)
  blocking collectives  160 us (35%)
  matrix products  22.6 us (5%)
  between operations  14.8 us (3%)
  other arithmetic  8.95 us (2%)
  local copies, waits for them, and re-layouts  8.09 us (2%)
    reduce_scatter x1, waiting for transfers between devices, on_device(): lax.psum_scatter(score_scale * lax.dot_general(dlogit, query_embed, (((0,...  127 us
    psum x1, waiting for transfers between devices, on_device(): lax.psum((query_in_part, query_out_part, item_in_part, item_out_part), ('...  116 us
    unnamed x2, blocking collectives  78 us
    all_gather x1, blocking collectives, on_device(): lax.all_gather(item_embed, ('dp', 'grp'), axis=0, tiled=True)  43.9 us
    psum x1, blocking collectives, on_device(): weight_total = lax.psum(weight_part, ('dp', 'grp'))  38.4 us
  transfers between devices with their start and end apart: 2, of which 2 were waited for; matrix products, arithmetic and copies ran while one was open for 2% of the time, Pallas kernels for 0%

commit v1 on v0

--- a/solution.py
+++ b/solution.py
@@ -102,7 +102,7 @@
         item_features, item_pre, item_hidden, item_w_out, item_grad
     )
     query_in_sum, query_out_sum, item_in_sum, item_out_sum = lax.psum(
-        (query_in_part, query_out_part, item_in_part, item_out_part), ("dp", "grp")
+        lax.psum((query_in_part, query_out_part, item_in_part, item_out_part), "grp"), "dp"
     )
     factor = loss_scale / weight_total
     return (

time: 458 us -> 550 us (1.20)
  waiting for transfers between devices: 243 us -> 329 us
  blocking collectives: 160 us -> 166 us
    psum x1 -> x2, waiting for transfers between devices: 116 us -> 202 us  [the longest x1 174 us: on_device(): lax.psum(lax.psum((query_in_part, query_out_part, item_in_part, item_out_...]
    psum x1, blocking collectives: 38.4 us -> 44.2 us  [on_device(): weight_total = lax.psum(weight_part, ('dp', 'grp'))]
  transfers between devices with their start and end apart: 2 -> 3, of which waited for: 2 -> 3; matrix products, arithmetic and copies ran while one was open for 2% -> 2% of each run, Pallas kernels for 0% -> 0%
where the time goes in v1:
time: 550 us; the launch traced here: 549 us
  waiting for transfers between devices  329 us (60%)
  blocking collectives  166 us (30%)
  matrix products  22.6 us (4%)
  between operations  14.5 us (3%)
  other arithmetic  8.95 us (2%)
  local copies, waits for them, and re-layouts  8.09 us (1%)
    psum x1, waiting for transfers between devices, on_device(): lax.psum(lax.psum((query_in_part, query_out_part, item_in_part, item_out_...  174 us
    reduce_scatter x1, waiting for transfers between devices, on_device(): lax.psum_scatter(score_scale * lax.dot_general(dlogit, query_embed, (((0,...  127 us
    unnamed x2, blocking collectives  78 us
    psum x1, blocking collectives, on_device(): weight_total = lax.psum(weight_part, ('dp', 'grp'))  44.2 us
    all_gather x1, blocking collectives, on_device(): lax.all_gather(item_embed, ('dp', 'grp'), axis=0, tiled=True)  43.9 us
    psum x1, waiting for transfers between devices, on_device(): lax.psum((query_in_part, query_out_part, item_in_part, item_out_part), 'g...  28.4 us
  transfers between devices with their start and end apart: 3, of which 3 were waited for; matrix products, arithmetic and copies ran while one was open for 2% of the time, Pallas kernels for 0%

profile of v1, /device:TPU:0, one launch (start us, length us, event | category | flops | bytes accessed | tf_op | source)
XLA Modules:
  0.0 549.1 jit_solution(13812481999312535425)
XLA Ops:
  7.2 1.6 fusion.16
  8.8 1.2 convolution_convert_fusion.1
  10.0 43.9 %all_gather.10 = bf16[512,256]{1,0:T(8,128)(2,1)S(1)} all-gather(bf16[16,256]{1,0:T(8,128)(2,1)S(1)} %convolution_convert_fusion.1), channel_id=1, replica_groups=mesh['dp'=16,'grp'=2] {'dp','grp'}, dimensions={0}, use_global_device_ids=true | all-gather | bytes 270336 | tf_op jit(solution)/shard_map/all_gather | solution.py:75
  54.0 0.8 dynamic-update-slice
  54.8 36.8 %all-reduce = s32[512]{0:T(512)S(1)} all-reduce(s32[512]{0:T(512)S(1)} %dynamic-update-slice), channel_id=1, replica_groups=mesh['dp'=16,'grp'=2] {'dp','grp'}, use_global_device_ids=true, to_apply=%add | all-reduce | flops 512 | bytes 4096
  91.6 0.8 dynamic-update-slice.1
  92.5 41.1 %all-reduce.1 = bf16[512]{0:T(512)(128)(2,1)S(1)} all-reduce(bf16[512]{0:T(512)(128)(2,1)S(1)} %dynamic-update-slice.1), channel_id=1, replica_groups=mesh['dp'=16,'grp'=2] {'dp','grp'}, use_global_device_ids=true, to_apply=%add.1 | all-reduce | flops 512 | bytes 2048
  133.6 4.8 multiply_convert_fusion.1
  138.4 0.7 convolution_convert_fusion
  140.1 0.8 fusion.15
  141.8 1.2 convolution_multiply_fusion.1
  143.7 1.1 copy-done.8
  144.7 1.7 fusion.17
  146.5 6.1 %convolution_bitcast_fusion.1 = f32[512,1024]{0,1:T(8,128)} fusion(bf16[1024,512]{1,0:T(8,128)(2,1)S(1)} %copy-done, f32[1024,1024]{1,0:T(8,128)} %get-tuple-element.17, bf16[1024,256]{1,0:T(8,128)(2,1)S(1)} %fusion.2, bf16[1024,256]{1,0:T(8,128)(2,1)S(1)} %copy-done.6), kind=kOutput, calls=%fused_computation.13 | convolution fusion | flops 1620049920 | bytes 8388608 | tf_op jit(solution)/shard_map/dot_general | solution.py:26
  152.5 126.7 %reduce-scatter.2.cloned.1.call-done = f32[16,256]{1,0:T(8,128)} async-done(((f32[512,256]{1,0:T(8,128)}), f32[16,256]{1,0:T(8,128)}) %reduce-scatter.2.cloned.1.call-update) | async-done | bytes 16400 | tf_op jit(solution)/shard_map/reduce_scatter | solution.py:89
  279.2 2.7 convolution_bitcast_fusion
  282.0 1.3 fusion.9
  283.4 28.4 %all-reduce.9.cloned.1.call-done = (f32[512,1024]{0,1:T(8,128)}, f32[1024,256]{1,0:T(8,128)}, f32[512,1024]{0,1:T(8,128)}, f32[1024,256]{1,0:T(8,128)}) async-done(((f32[512,1024]{0,1:T(8,128)}, f32[1024,256]{1,0:T(8,128)}, f32[512,1024]{0,1:T(8,128)}, f32[1024,256]{1,0:T(8,128)}), (f32[512,1024]{0,1:T(8,128)}, f32[1024,256]{1,0:T(8,128)}, f32[512,1024]{0,1:T(8,128)}, ...) | async-done | bytes 6291472 | tf_op jit(solution)/shard_map/psum | solution.py:105
  312.4 44.2 %psum.65 = f32[]{:T(128)} all-reduce(f32[]{:T(128)} %convert_reduce_fusion), channel_id=1, replica_groups=mesh['dp'=16,'grp'=2] {'dp','grp'}, use_global_device_ids=true, to_apply=%region_6.7 | all-reduce | flops 1 | bytes 8 | tf_op jit(solution)/shard_map/psum | solution.py:71
  357.2 173.6 %all-reduce.7.cloned.1.call-done = (f32[512,1024]{0,1:T(8,128)}, f32[1024,256]{1,0:T(8,128)}, f32[512,1024]{0,1:T(8,128)}, f32[1024,256]{1,0:T(8,128)}) async-done(((f32[512,1024]{0,1:T(8,128)}, f32[1024,256]{1,0:T(8,128)}, f32[512,1024]{0,1:T(8,128)}, f32[1024,256]{1,0:T(8,128)}), (f32[512,1024]{0,1:T(8,128)}, f32[1024,256]{1,0:T(8,128)}, f32[512,1024]{0,1:T(8,128)}, ...) | async-done | bytes 6291472 | tf_op jit(solution)/shard_map/psum | solution.py:104
  530.8 4.0 broadcast_multiply_fusion
  534.9 2.9 copy.14
  537.7 1.8 copy.15
  539.5 3.0 broadcast_multiply_fusion.2
  (33 shorter events, 3.2 us)
Async XLA Ops:
  7.2 126.5 %copy-start = (bf16[1024,512]{1,0:T(8,128)(2,1)S(1)}, bf16[1024,512]{1,0:T(8,128)(2,1)}, u32[]{:S(2)}) copy-start(bf16[1024,512]{1,0:T(8,128)(2,1)} %param.10) | copy-start | bytes 3145732
  7.2 272.0 %reduce-scatter.2.cloned.1.call-start = ((), (), s32[]{:S(2)}) async-start(), calls=%async_computation.1 | async-start | bytes 540672 | tf_op jit(solution)/shard_map/reduce_scatter | solution.py:89
  133.6 4.8 copy-start.6
  138.4 1.3 copy-start.7
  138.4 1.3 copy-start.4
  140.0 0.8 copy-start.5
  143.1 168.6 %all-reduce.9.cloned.1.call-start = ((), (), s32[]{:S(2)}) async-start(), calls=%async_computation.3 | async-start | bytes 12582912 | tf_op jit(solution)/shard_map/psum | solution.py:105
  143.2 1.6 copy-start.8
  146.5 132.8 %copy-start.1 = (bf16[1024,256]{1,0:T(8,128)(2,1)S(1)}, bf16[1024,256]{1,0:T(8,128)(2,1)}, u32[]{:S(2)}) copy-start(bf16[1024,256]{1,0:T(8,128)(2,1)} %param.19) | copy-start | bytes 1572868
  146.5 132.8 %copy-start.2 = (bf16[16,512]{1,0:T(8,128)(2,1)S(1)}, bf16[16,512]{1,0:T(8,128)(2,1)}, u32[]{:S(2)}) copy-start(bf16[16,512]{1,0:T(8,128)(2,1)} %param.13) | copy-start | bytes 49156
  279.2 2.8 copy-start.3
  283.3 247.5 %all-reduce.7.cloned.1.call-start = ((), (), s32[]{:S(2)}) async-start(), calls=%async_computation.2 | async-start | bytes 12582912 | tf_op jit(solution)/shard_map/psum | solution.py:104
Sparse Core Ops, SparseCore 0:
  143.2 135.9 reduce-scatter.1
  283.4 28.2 all-reduce.8
  318.2 212.5 all-reduce.6
